TPU v7x, 32 devices: a whole 2x2x4 slice. The times are simulated.
32 devices in a mesh: rep: 4 (over x, core), fsdp: 4 (over z), seq: 2 (over y).
Axes of the slice: x: 2, y: 2, z: 4, core: 2. Of those that a mesh axis runs over, the one named last changes fastest.
Arguments:
- tokens: bfloat16 [16, 592, 1024], P(('rep', 'fsdp'), 'seq'), may hold values from -6 to 6
- slot_mask: int32 [16], P(('rep', 'fsdp')), may hold values 0 or 1
- cotangent: bfloat16 [16, 592, 1024], P(('rep', 'fsdp'), 'seq'), may hold values from -6 to 6
- w_qkv: float32 [1024, 3072], P('fsdp'), may hold values from -0.25 to 0.25
- w_out: float32 [1024, 1024], P('fsdp'), may hold values from -0.75 to 0.75
- w_fc1: float32 [1024, 4096], P('fsdp'), may hold values from -0.1875 to 0.1875
- w_fc2: float32 [4096, 1024], P('fsdp'), may hold values from -0.125 to 0.125
- ln_gains: float32 [2, 1024], P(None, 'fsdp'), may hold values from 0.5 to 1.5
- biases: float32 [6, 1024], P(None, 'fsdp'), may hold values from -2 to 2
- fc1_bias: float32 [4096], P('fsdp'), may hold values from -2 to 2
Outputs:
- output: bfloat16 [16, 592, 1024], P(('rep', 'fsdp'), 'seq')
- grad_tokens: bfloat16 [16, 592, 1024], P(('rep', 'fsdp'), 'seq')
- grad_w_qkv: float32 [1024, 3072], P('fsdp')
- grad_w_out: float32 [1024, 1024], P('fsdp')
- grad_w_fc1: float32 [1024, 4096], P('fsdp')
- grad_w_fc2: float32 [4096, 1024], P('fsdp')
- grad_ln_gains: float32 [2, 1024], P(None, 'fsdp')
- grad_biases: float32 [6, 1024], P(None, 'fsdp')
- grad_fc1_bias: float32 [4096], P('fsdp')
All inputs are finite; a program needn't handle non-finite values. No bound on the sum of `slot_mask` on one device may be relied on, other than what follows from the above.
Results may differ from a plain program's by a relative error of at most 0.02.
The roundings to bfloat16 on the way count: a program that leaves them out, or rounds other values in their place, can miss the bound.
Values may be sent and summed in bfloat16 or wider, within the bound.
No kernel may reach another device: no remote copies, remote signals or barrier semaphores. Data moves between devices by JAX's collectives and lax.ppermute only.
A program may use at most 192 MiB of HBM per device.

v0:
```python
import jax
import jax.numpy as jnp
from jax import lax
from jax.sharding import PartitionSpec as P

HEADS = 16
HEAD_DIM = 64
IMG_TOK = 577
EPSILON = 1e-05
NEGATIVE = -1e30


def normalize(inputs, gain_row, shift_row):
    center = inputs - jnp.mean(inputs, axis=-1, keepdims=True)
    inverse = lax.rsqrt(jnp.mean(center * center, axis=-1, keepdims=True) + EPSILON)
    scaled = center * inverse
    return (scaled * gain_row + shift_row, scaled, inverse)


def norm_back(grad_in, scaled, inverse, gain_row):
    weighted = grad_in * gain_row
    return inverse * (
        weighted
        - jnp.mean(weighted, axis=-1, keepdims=True)
        - scaled * jnp.mean(weighted * scaled, axis=-1, keepdims=True)
    )


def across_rows(left_rows, right_rows):
    return lax.dot_general(
        left_rows, right_rows, (((0,), (0,)), ((), ())), preferred_element_type=jnp.float32
    )


def times_transposed(left_rows, right_rows):
    return lax.dot_general(
        left_rows, right_rows, (((1,), (1,)), ((), ())), preferred_element_type=jnp.float32
    )


def split_heads(matrix):
    return matrix.reshape(matrix.shape[0], HEADS, HEAD_DIM)


def masked_scores(query_rows, key_rows):
    scores = jnp.einsum(
        "qhd,khd->hqk",
        split_heads(query_rows),
        split_heads(key_rows),
        preferred_element_type=jnp.float32,
    )
    valid_keys = jnp.arange(key_rows.shape[0]) < IMG_TOK
    return jnp.where(valid_keys[None, None, :], scores, NEGATIVE)


def attend_slot(blocks_in):
    query_rows, key_rows, value_rows = blocks_in
    scores = masked_scores(query_rows, key_rows)
    highest = jnp.max(scores, axis=-1, keepdims=True)
    exponent = jnp.exp(scores - highest)
    total_sum = jnp.sum(exponent, axis=-1, keepdims=True)
    weights = (exponent / total_sum).astype(jnp.bfloat16)
    mixed_rows = jnp.einsum(
        "hqk,khd->qhd", weights, split_heads(value_rows), preferred_element_type=jnp.float32
    )
    return (mixed_rows.reshape(query_rows.shape[0], -1), highest + jnp.log(total_sum))


def attend_back(blocks_in):
    query_rows, key_rows, value_rows, log_total, grad_rows = blocks_in
    scores = masked_scores(query_rows, key_rows)
    probability = jnp.exp(scores - log_total)
    grad_heads = split_heads(grad_rows)
    grad_probs = jnp.einsum(
        "qhd,khd->hqk", grad_heads, split_heads(value_rows), preferred_element_type=jnp.float32
    )
    inner_sum = jnp.sum(probability * grad_probs, axis=-1, keepdims=True)
    grad_scores = (probability * (grad_probs - inner_sum)).astype(jnp.bfloat16)
    grad_query = jnp.einsum(
        "hqk,khd->qhd", grad_scores, split_heads(key_rows), preferred_element_type=jnp.float32
    )
    grad_key = jnp.einsum(
        "hqk,qhd->khd", grad_scores, split_heads(query_rows), preferred_element_type=jnp.float32
    )
    grad_value = jnp.einsum(
        "hqk,qhd->khd",
        probability.astype(jnp.bfloat16),
        grad_heads,
        preferred_element_type=jnp.float32,
    )
    key_count = key_rows.shape[0]
    return (
        grad_query.reshape(query_rows.shape[0], -1),
        grad_key.reshape(key_count, -1),
        grad_value.reshape(key_count, -1),
    )


def on_device(tokens, slot_mask, cotangent, w_qkv, w_out, w_fc1, w_fc2, ln_gains, biases, fc1_bias):
    slot_count, row_count, feature_width = tokens.shape
    low_qkv = w_qkv.astype(jnp.bfloat16)
    low_out = w_out.astype(jnp.bfloat16)
    low_fc1 = w_fc1.astype(jnp.bfloat16)
    low_fc2 = w_fc2.astype(jnp.bfloat16)
    low_gains = ln_gains.astype(jnp.bfloat16)
    low_biases = biases.astype(jnp.bfloat16)
    low_fc1_bias = fc1_bias.astype(jnp.bfloat16)
    gathered = (
        lax.all_gather(low_qkv, "fsdp", axis=0, tiled=True),
        lax.all_gather(low_out, "fsdp", axis=0, tiled=True),
        lax.all_gather(low_fc1, "fsdp", axis=0, tiled=True),
        lax.all_gather(low_fc2, "fsdp", axis=0, tiled=True),
        lax.all_gather(low_gains, "fsdp", axis=1, tiled=True),
        lax.all_gather(low_biases, "fsdp", axis=1, tiled=True),
        lax.all_gather(low_fc1_bias, "fsdp", axis=0, tiled=True),
    )
    big_qkv, big_out, big_fc1, big_fc2, gain_rows, bias_rows, fc1_shift = gathered
    gain_values = gain_rows.astype(jnp.float32)
    shift_values = bias_rows.astype(jnp.float32)
    hidden_shift = fc1_shift.astype(jnp.float32)
    head_scale = HEAD_DIM ** (-0.5)
    positions = lax.axis_index("seq") * row_count + jnp.arange(row_count)
    keep_mask = (
        slot_mask.astype(jnp.float32)[:, None] * (positions < IMG_TOK).astype(jnp.float32)[None, :]
    )
    keep_mask = keep_mask.reshape(-1, 1)
    inputs = tokens.astype(jnp.float32).reshape(-1, feature_width)
    normed_full, scaled_one, inverse_one = normalize(inputs, gain_values[0], shift_values[0])
    normed = normed_full.astype(jnp.bfloat16)
    joined = jnp.dot(normed, big_qkv, preferred_element_type=jnp.float32)
    queries = ((joined[:, :feature_width] + shift_values[1]) * head_scale).astype(jnp.bfloat16)
    keys_local = (
        joined[:, feature_width : 2 * feature_width]
        .astype(jnp.bfloat16)
        .reshape(slot_count, row_count, feature_width)
    )
    values_local = (
        (joined[:, 2 * feature_width :] + shift_values[2])
        .astype(jnp.bfloat16)
        .reshape(slot_count, row_count, feature_width)
    )
    slot_queries = queries.reshape(slot_count, row_count, feature_width)
    keys_all, values_all = (
        lax.all_gather(keys_local, "seq", axis=1, tiled=True),
        lax.all_gather(values_local, "seq", axis=1, tiled=True),
    )
    mixed_rows, log_total = lax.map(attend_slot, (slot_queries, keys_all, values_all))
    mixed_low = mixed_rows.reshape(-1, feature_width).astype(jnp.bfloat16)
    middle = inputs + (
        jnp.dot(mixed_low, big_out, preferred_element_type=jnp.float32) + shift_values[3]
    )
    normed_two_full, scaled_two, inverse_two = normalize(middle, gain_values[1], shift_values[4])
    normed_two = normed_two_full.astype(jnp.bfloat16)
    hidden = jnp.dot(normed_two, big_fc1, preferred_element_type=jnp.float32) + hidden_shift
    gate_values = jax.nn.sigmoid(1.702 * hidden)
    active = (hidden * gate_values).astype(jnp.bfloat16)
    result = jnp.dot(active, big_fc2, preferred_element_type=jnp.float32) + shift_values[5]
    output = ((middle + result) * keep_mask).astype(jnp.bfloat16).reshape(tokens.shape)
    again = (
        lax.all_gather(low_qkv, "fsdp", axis=0, tiled=True),
        lax.all_gather(low_out, "fsdp", axis=0, tiled=True),
        lax.all_gather(low_fc1, "fsdp", axis=0, tiled=True),
        lax.all_gather(low_fc2, "fsdp", axis=0, tiled=True),
        lax.all_gather(low_gains, "fsdp", axis=1, tiled=True),
        lax.all_gather(low_biases, "fsdp", axis=1, tiled=True),
        lax.all_gather(low_fc1_bias, "fsdp", axis=0, tiled=True),
    )
    back_qkv, back_out, back_fc1, back_fc2, back_gain_rows = (
        again[0],
        again[1],
        again[2],
        again[3],
        again[4],
    )
    back_gains = back_gain_rows.astype(jnp.float32)
    incoming = cotangent.astype(jnp.float32).reshape(-1, feature_width) * keep_mask
    grad_result = incoming.astype(jnp.bfloat16)
    grad_fc2 = across_rows(active, grad_result)
    grad_shift_five = jnp.sum(grad_result.astype(jnp.float32), axis=0)
    grad_active = times_transposed(grad_result, back_fc2)
    grad_hidden = (
        grad_active * (gate_values + 1.702 * hidden * gate_values * (1.0 - gate_values))
    ).astype(jnp.bfloat16)
    grad_fc1 = across_rows(normed_two, grad_hidden)
    grad_hidden_shift = jnp.sum(grad_hidden.astype(jnp.float32), axis=0)
    grad_normed_two = times_transposed(grad_hidden, back_fc1)
    grad_gain_two = jnp.sum(grad_normed_two * scaled_two, axis=0)
    grad_shift_four = jnp.sum(grad_normed_two, axis=0)
    grad_middle = incoming + norm_back(grad_normed_two, scaled_two, inverse_two, back_gains[1])
    grad_branch = grad_middle.astype(jnp.bfloat16)
    grad_out = across_rows(mixed_low, grad_branch)
    grad_shift_three = jnp.sum(grad_branch.astype(jnp.float32), axis=0)
    grad_mixed = times_transposed(grad_branch, back_out).astype(jnp.bfloat16)
    grad_query, key_part, value_part = lax.map(
        attend_back,
        (
            slot_queries,
            keys_all,
            values_all,
            log_total,
            grad_mixed.reshape(slot_count, row_count, feature_width),
        ),
    )
    grad_keys, grad_values = (
        lax.psum_scatter(
            key_part.astype(jnp.bfloat16), "seq", scatter_dimension=1, tiled=True
        ).astype(jnp.float32),
        lax.psum_scatter(
            value_part.astype(jnp.bfloat16), "seq", scatter_dimension=1, tiled=True
        ).astype(jnp.float32),
    )
    query_grad_low = (grad_query.astype(jnp.bfloat16) * head_scale).reshape(-1, feature_width)
    key_grad_low = grad_keys.astype(jnp.bfloat16).reshape(-1, feature_width)
    value_grad_low = grad_values.astype(jnp.bfloat16).reshape(-1, feature_width)
    grad_joined = jnp.concatenate([query_grad_low, key_grad_low, value_grad_low], axis=1)
    grad_qkv = across_rows(normed, grad_joined)
    grad_shift_one = jnp.sum(query_grad_low.astype(jnp.float32), axis=0)
    grad_shift_two = jnp.sum(value_grad_low.astype(jnp.float32), axis=0)
    grad_normed = times_transposed(grad_joined, back_qkv)
    grad_gain_one = jnp.sum(grad_normed * scaled_one, axis=0)
    grad_shift_zero = jnp.sum(grad_normed, axis=0)
    grad_inputs = grad_middle + norm_back(grad_normed, scaled_one, inverse_one, back_gains[0])
    grad_tokens = grad_inputs.astype(jnp.bfloat16).reshape(tokens.shape)
    grad_gains = jnp.stack([grad_gain_one, grad_gain_two])
    grad_shifts = jnp.stack(
        [
            grad_shift_zero,
            grad_shift_one,
            grad_shift_two,
            grad_shift_three,
            grad_shift_four,
            grad_shift_five,
        ]
    )
    shards = (
        lax.psum_scatter(
            grad_qkv.astype(jnp.bfloat16), "fsdp", scatter_dimension=0, tiled=True
        ).astype(jnp.float32),
        lax.psum_scatter(
            grad_out.astype(jnp.bfloat16), "fsdp", scatter_dimension=0, tiled=True
        ).astype(jnp.float32),
        lax.psum_scatter(
            grad_fc1.astype(jnp.bfloat16), "fsdp", scatter_dimension=0, tiled=True
        ).astype(jnp.float32),
        lax.psum_scatter(
            grad_fc2.astype(jnp.bfloat16), "fsdp", scatter_dimension=0, tiled=True
        ).astype(jnp.float32),
        lax.psum_scatter(
            grad_gains.astype(jnp.bfloat16), "fsdp", scatter_dimension=1, tiled=True
        ).astype(jnp.float32),
        lax.psum_scatter(
            grad_shifts.astype(jnp.bfloat16), "fsdp", scatter_dimension=1, tiled=True
        ).astype(jnp.float32),
        lax.psum_scatter(
            grad_hidden_shift.astype(jnp.bfloat16), "fsdp", scatter_dimension=0, tiled=True
        ).astype(jnp.float32),
    )
    summed = (
        lax.psum(shards[0].astype(jnp.bfloat16), ("rep", "seq")).astype(jnp.float32),
        lax.psum(shards[1].astype(jnp.bfloat16), ("rep", "seq")).astype(jnp.float32),
        lax.psum(shards[2].astype(jnp.bfloat16), ("rep", "seq")).astype(jnp.float32),
        lax.psum(shards[3].astype(jnp.bfloat16), ("rep", "seq")).astype(jnp.float32),
        lax.psum(shards[4].astype(jnp.bfloat16), ("rep", "seq")).astype(jnp.float32),
        lax.psum(shards[5].astype(jnp.bfloat16), ("rep", "seq")).astype(jnp.float32),
        lax.psum(shards[6].astype(jnp.bfloat16), ("rep", "seq")).astype(jnp.float32),
    )
    return (
        output,
        grad_tokens,
        summed[0],
        summed[1],
        summed[2],
        summed[3],
        summed[4],
        summed[5],
        summed[6],
    )


def solution(mesh):
    return jax.shard_map(
        on_device,
        mesh=mesh,
        in_specs=(
            P(("rep", "fsdp"), "seq", None),
            P(("rep", "fsdp")),
            P(("rep", "fsdp"), "seq", None),
            P("fsdp", None),
            P("fsdp", None),
            P("fsdp", None),
            P("fsdp", None),
            P(None, "fsdp"),
            P(None, "fsdp"),
            P("fsdp"),
        ),
        out_specs=(
            P(("rep", "fsdp"), "seq", None),
            P(("rep", "fsdp"), "seq", None),
            P("fsdp", None),
            P("fsdp", None),
            P("fsdp", None),
            P("fsdp", None),
            P(None, "fsdp"),
            P(None, "fsdp"),
            P("fsdp"),
        ),
        check_vma=False,
    )
```

profile of v0, /device:TPU:0, one launch (start us, length us, event | category | flops | bytes accessed | tf_op | source)
XLA Modules:
  0.0 1236.4 jit_solution(1024592312134364579)
XLA Ops:
  10.7 12.6 %all_gather.32 = bf16[2,1024]{1,0:T(2,128)(2,1)S(1)} all-gather(bf16[2,256]{1,0:T(2,128)(2,1)S(1)} %convert_element_type.210), channel_id=1, replica_groups=mesh['rep'=4,'fsdp'=4,'seq'=2] {'fsdp'}, dimensions={1}, use_global_device_ids=true | all-gather | bytes 5120 | tf_op jit(solution)/shard_map/all_gather | solution.py:113
  23.3 14.3 %all_gather.33 = bf16[6,1024]{1,0:T(8,128)(2,1)S(1)} all-gather(bf16[6,256]{1,0:T(8,128)(2,1)S(1)} %convert_element_type.212), channel_id=1, replica_groups=mesh['rep'=4,'fsdp'=4,'seq'=2] {'fsdp'}, dimensions={1}, use_global_device_ids=true | all-gather | bytes 15360 | tf_op jit(solution)/shard_map/all_gather | solution.py:114
  38.1 90.8 %all-gather.9.cloned.1.call-done = bf16[1024,3072]{1,0:T(8,128)(2,1)} async-done(((bf16[256,3072]{1,0:T(8,128)(2,1)}), bf16[1024,3072]{1,0:T(8,128)(2,1)}) %all-gather.9.cloned.1.call-update) | async-done | bytes 6291472 | tf_op jit(solution)/shard_map/all_gather | solution.py:109
  128.9 5.0 fusion.53
  149.5 11.9 all_gather.39
  163.7 19.9 %all-gather.17.cloned.1.call-done = bf16[592,1024]{1,0:T(8,128)(2,1)} async-done(((bf16[296,1024]{1,0:T(8,128)(2,1)}), bf16[592,1024]{1,0:T(8,128)(2,1)}) %all-gather.17.cloned.1.call-update) | async-done | bytes 1212432 | tf_op jit(solution)/shard_map/all_gather | solution.py:145
  193.1 4.5 fusion.20
  197.6 33.4 %all-gather.11.cloned.1.call-done = bf16[1024,1024]{1,0:T(8,128)(2,1)} async-done(((bf16[256,1024]{1,0:T(8,128)(2,1)}), bf16[1024,1024]{1,0:T(8,128)(2,1)}) %all-gather.11.cloned.1.call-update) | async-done | bytes 2097168 | tf_op jit(solution)/shard_map/all_gather | solution.py:110
  234.1 147.3 %all-gather.13.cloned.1.call-done = bf16[1024,4096]{1,0:T(8,128)(2,1)} async-done(((bf16[256,4096]{1,0:T(8,128)(2,1)}), bf16[1024,4096]{1,0:T(8,128)(2,1)}) %all-gather.13.cloned.1.call-update) | async-done | bytes 8388624 | tf_op jit(solution)/shard_map/all_gather | solution.py:111
  381.4 8.5 convolution_add_fusion
  389.9 141.4 %all-gather.15.cloned.1.call-done = bf16[4096,1024]{1,0:T(8,128)(2,1)} async-done(((bf16[1024,1024]{1,0:T(8,128)(2,1)}), bf16[4096,1024]{1,0:T(8,128)(2,1)}) %all-gather.15.cloned.1.call-update) | async-done | bytes 8388624 | tf_op jit(solution)/shard_map/all_gather | solution.py:112
  531.3 9.1 fusion.61
  549.0 8.5 fusion.9
  557.6 6.2 copy.37
  567.0 9.8 multiply_reduce_fusion
  576.8 6.6 multiply_convert_fusion
  586.4 6.2 copy.35
  600.4 5.6 fusion.60
  610.9 5.2 reduce-scatter.25.cloned.1.call-done
  620.0 7.4 convolution_convert_fusion.2
  628.4 9.7 convolution_convert_fusion
  638.1 8.8 convolution_convert_fusion.1
  647.2 6.6 fusion.33
  655.7 7.2 reduce-scatter.17.cloned.1.call-done
  662.8 112.4 %reduce-scatter.15.cloned.1.call-done = bf16[256,3072]{1,0:T(8,128)(2,1)} async-done(((bf16[1024,3072]{1,0:T(8,128)(2,1)}), bf16[256,3072]{1,0:T(8,128)(2,1)}) %reduce-scatter.15.cloned.1.call-update) | async-done | bytes 1572880 | tf_op jit(solution)/shard_map/reduce_scatter | solution.py:236
  775.2 147.5 %reduce-scatter.21.cloned.1.call-done = bf16[1024,1024]{1,0:T(8,128)(2,1)} async-done(((bf16[4096,1024]{1,0:T(8,128)(2,1)}), bf16[1024,1024]{1,0:T(8,128)(2,1)}) %reduce-scatter.21.cloned.1.call-update) | async-done | bytes 2097168 | tf_op jit(solution)/shard_map/reduce_scatter | solution.py:245
  922.7 147.6 %reduce-scatter.19.cloned.1.call-done = bf16[256,4096]{1,0:T(8,128)(2,1)} async-done(((bf16[1024,4096]{1,0:T(8,128)(2,1)}), bf16[256,4096]{1,0:T(8,128)(2,1)}) %reduce-scatter.19.cloned.1.call-update) | async-done | bytes 2097168 | tf_op jit(solution)/shard_map/reduce_scatter | solution.py:242
  1072.1 11.4 all-reduce
  1083.6 8.6 fusion.25
  1094.5 18.9 %reduce-scatter.23.cloned.1.call-done = bf16[6,256]{1,0:T(8,128)(2,1)} async-done(((bf16[6,1024]{1,0:T(8,128)(2,1)}), bf16[6,256]{1,0:T(8,128)(2,1)}) %reduce-scatter.23.cloned.1.call-update) | async-done | bytes 3088 | tf_op jit(solution)/shard_map/reduce_scatter | solution.py:251
  1113.4 14.1 %all-reduce.1 = (bf16[2,256]{1,0:T(2,128)(2,1)S(1)}, bf16[6,256]{1,0:T(8,128)(2,1)S(1)}, bf16[1024]{0:T(1024)(128)(2,1)S(1)}) all-reduce(bf16[2,256]{1,0:T(2,128)(2,1)S(1)} %copy.40, bf16[6,256]{1,0:T(8,128)(2,1)} %reduce-scatter.23.cloned.1.call-done, ...), channel_id=1, replica_groups=mesh['rep'=4,'fsdp'=4,'seq'=2] {'rep','seq'}, use_global_device_ids=true, to_apply=%region_24.25 | all-reduce | flops 3072 | bytes 12288 | tf_op jit(solution)/shard_map/psum | solution.py:263
  1129.2 91.0 %all-reduce.5.cloned.1.call-done = (bf16[256,3072]{1,0:T(8,128)(2,1)}, bf16[256,1024]{1,0:T(8,128)(2,1)}, bf16[256,4096]{1,0:T(8,128)(2,1)}, bf16[1024,1024]{1,0:T(8,128)(2,1)}) async-done(((bf16[256,3072]{1,0:T(8,128)(2,1)}, bf16[256,1024]{1,0:T(8,128)(2,1)}, bf16[256,4096]{1,0:T(8,128)(2,1)}, bf16[1024,1024]{1,0:T(8,128)(2,1)}), (bf16[256,3072]{1,0:T(8,128)(2,1)}, bf16[256,1024]{1,0:T(8,128)(2,1)}, ...) | async-done | bytes 6291472 | tf_op jit(solution)/shard_map/psum | solution.py:259
  (145 shorter events, 82.8 us)
Async XLA Ops:
  7.2 3.5 copy-start.19
  7.2 3.5 copy-start.17
  7.2 30.4 %copy-start.2 = (bf16[1,296,1024]{2,1,0:T(8,128)(2,1)S(1)}, bf16[1,296,1024]{2,1,0:T(8,128)(2,1)}, u32[]{:S(2)}) copy-start(bf16[1,296,1024]{2,1,0:T(8,128)(2,1)} %param.10) | copy-start | bytes 1818628
  7.2 121.7 %all-gather.9.cloned.1.call-start = ((), (), s32[]{:S(2)}) async-start(), calls=%async_computation.8 | async-start | bytes 7864320 | tf_op jit(solution)/shard_map/all_gather | solution.py:109
  10.6 151.2 %all-gather.19.cloned.1.call-start = ((), (), s32[]{:S(2)}) async-start(), calls=%async_computation.18 | async-start | bytes 1818624 | tf_op jit(solution)/shard_map/all_gather | solution.py:144
  136.7 46.9 %all-gather.17.cloned.1.call-start = ((), (), s32[]{:S(2)}) async-start(), calls=%async_computation.17 | async-start | bytes 1818624 | tf_op jit(solution)/shard_map/all_gather | solution.py:145
  136.8 3.0 copy-start.13
  139.7 91.3 %all-gather.11.cloned.1.call-start = ((), (), s32[]{:S(2)}) async-start(), calls=%async_computation.9 | async-start | bytes 2621440 | tf_op jit(solution)/shard_map/all_gather | solution.py:110
  140.7 240.7 %all-gather.13.cloned.1.call-start = ((), (), s32[]{:S(2)}) async-start(), calls=%async_computation.10 | async-start | bytes 10485760 | tf_op jit(solution)/shard_map/all_gather | solution.py:111
  144.8 386.4 %all-gather.15.cloned.1.call-start = ((), (), s32[]{:S(2)}) async-start(), calls=%async_computation.11 | async-start | bytes 10485760 | tf_op jit(solution)/shard_map/all_gather | solution.py:112
  148.7 457.3 %reduce-scatter.27.cloned.1.call-start = ((), (), s32[]{:S(2)}) async-start(), calls=%async_computation.20 | async-start | bytes 1818624
  161.7 24.3 %copy-start.5 = (bf16[296,1024]{0,1:T(8,128)(2,1)}, bf16[296,1024]{0,1:T(8,128)(2,1)S(1)}, u32[]{:S(2)}) copy-start(bf16[296,1024]{0,1:T(8,128)(2,1)S(1)} %copy.32) | copy-start | bytes 1818628
  188.2 4.9 copy-start
  188.2 4.9 copy-start.7
  531.3 9.1 copy-start.20
  540.3 3.1 copy-start.22
  540.3 3.1 copy-start.14
  567.0 49.1 %reduce-scatter.25.cloned.1.call-start = ((), (), s32[]{:S(2)}) async-start(), calls=%async_computation.19 | async-start | bytes 1818624
  576.8 6.6 copy-start.6
  583.4 3.0 copy-start.1
  595.8 67.0 %reduce-scatter.17.cloned.1.call-start = ((), (), s32[]{:S(2)}) async-start(), calls=%async_computation.13 | async-start | bytes 2621440 | tf_op jit(solution)/shard_map/reduce_scatter | solution.py:239
  600.0 175.2 %reduce-scatter.15.cloned.1.call-start = ((), (), s32[]{:S(2)}) async-start(), calls=%async_computation.12 | async-start | bytes 7864320 | tf_op jit(solution)/shard_map/reduce_scatter | solution.py:236
  627.4 295.3 %reduce-scatter.21.cloned.1.call-start = ((), (), s32[]{:S(2)}) async-start(), calls=%async_computation.15 | async-start | bytes 10485760 | tf_op jit(solution)/shard_map/reduce_scatter | solution.py:245
  638.1 432.1 %reduce-scatter.19.cloned.1.call-start = ((), (), s32[]{:S(2)}) async-start(), calls=%async_computation.14 | async-start | bytes 10485760 | tf_op jit(solution)/shard_map/reduce_scatter | solution.py:242
  647.0 446.6 %reduce-scatter.29.cloned.1.call-start = ((), (), s32[]{:S(2)}) async-start(), calls=%async_computation.21 | async-start | bytes 327680
  654.7 458.6 %reduce-scatter.23.cloned.1.call-start = ((), (), s32[]{:S(2)}) async-start(), calls=%async_computation.16 | async-start | bytes 20480 | tf_op jit(solution)/shard_map/reduce_scatter | solution.py:251
  655.6 564.7 %all-reduce.5.cloned.1.call-start = ((), (), s32[]{:S(2)}) async-start(), calls=%async_computation.22 | async-start | bytes 12582912 | tf_op jit(solution)/shard_map/psum | solution.py:259
  1083.5 8.7 copy-start.16
  1083.5 8.7 copy-start.4
  1092.2 21.2 %dynamic-slice-start = ((bf16[4096]{0:T(1024)(128)(2,1)}, u32[]{:T(128)}), bf16[1024]{0:T(1024)(128)(2,1)S(1)}, s32[]{:S(2)}) async-start(bf16[4096]{0:T(1024)(128)(2,1)} %copy-done.16, u32[]{:T(128)} %multiply.49), calls=%async_computation.23 | async-start | bytes 4608
  1220.3 2.2 copy-start.12
  1224.7 2.5 copy-start.9
  (7 other events, 9.2 us)
Sparse Core Ops, SparseCore 0:
  10.7 118.1 all-gather.8
  136.8 21.4 all-gather.18
  160.4 23.1 all-gather.16
  185.0 45.9 all-gather.10
  233.0 148.3 all-gather.12
  383.4 147.8 all-gather.14
  567.1 20.3 reduce-scatter.26
  595.9 20.0 reduce-scatter.24
  618.9 43.8 reduce-scatter.16
  665.1 110.0 reduce-scatter.14
  777.6 144.9 reduce-scatter.20
  925.0 145.1 reduce-scatter.18
  1073.2 20.3 reduce-scatter.28
  1096.2 17.1 reduce-scatter.22
  1117.3 102.9 all-reduce.4
where the time goes:
time: 1240 us
  waiting for transfers between devices  963 us (78%)
  matrix products  109 us (9%)
  blocking collectives  64.3 us (5%)
  local copies, waits for them, and re-layouts  42.4 us (3%)
  other arithmetic  41.2 us (3%)
  between operations  15.9 us (1%)
    reduce_scatter x1, waiting for transfers between devices, on_device(): lax.psum_scatter(grad_fc1.astype(jnp.bfloat16), 'fsdp', scatter_dimension...  148 us
    reduce_scatter x1, waiting for transfers between devices, on_device(): lax.psum_scatter(grad_fc2.astype(jnp.bfloat16), 'fsdp', scatter_dimension...  148 us
    all_gather x1, waiting for transfers between devices, on_device(): lax.all_gather(low_fc1, 'fsdp', axis=0, tiled=True)  147 us
    all_gather x1, waiting for transfers between devices, on_device(): lax.all_gather(low_fc2, 'fsdp', axis=0, tiled=True)  141 us
    reduce_scatter x1, waiting for transfers between devices, on_device(): lax.psum_scatter(grad_qkv.astype(jnp.bfloat16), 'fsdp', scatter_dimension...  112 us
    psum x1, waiting for transfers between devices, on_device(): lax.psum(shards[0].astype(jnp.bfloat16), ('rep', 'seq')).astype(jnp.float32)  91 us
    all_gather x1, waiting for transfers between devices, on_device(): lax.all_gather(low_qkv, 'fsdp', axis=0, tiled=True)  90.8 us
    unnamed x58, local copies, waits for them, and re-layouts  33.7 us
  transfers between devices with their start and end apart: 15, of which 12 were waited for; matrix products, arithmetic and copies ran while one was open for 11% of the time, Pallas kernels for 0%

commit v1 on v0

--- a/solution.py
+++ b/solution.py
@@ -255,8 +255,13 @@
             grad_hidden_shift.astype(jnp.bfloat16), "fsdp", scatter_dimension=0, tiled=True
         ).astype(jnp.float32),
     )
+
+    def extend_islands(vector):
+        far_arr = jax.lax.psum(vector, "seq")
+        return jax.lax.psum(far_arr, "rep")
+
     summed = (
-        lax.psum(shards[0].astype(jnp.bfloat16), ("rep", "seq")).astype(jnp.float32),
+        extend_islands(shards[0].astype(jnp.bfloat16)).astype(jnp.float32),
         lax.psum(shards[1].astype(jnp.bfloat16), ("rep", "seq")).astype(jnp.float32),
         lax.psum(shards[2].astype(jnp.bfloat16), ("rep", "seq")).astype(jnp.float32),
         lax.psum(shards[3].astype(jnp.bfloat16), ("rep", "seq")).astype(jnp.float32),

time: 1240 us -> 1330 us (1.073)
  waiting for transfers between devices: 963 us -> 1050 us
    psum x1 -> x3, waiting for transfers between devices: 91 us -> 136 us  [the longest x1 87.3 us: on_device(): lax.psum(shards[1].astype(jnp.bfloat16), ('rep', 'seq')).astype(jnp.float32)]
    reduce_scatter x1, waiting for transfers between devices: 7.15 us -> 46.8 us  [on_device(): lax.psum_scatter(grad_out.astype(jnp.bfloat16), 'fsdp', scatter_dimension...]
    all_gather x1, waiting for transfers between devices: 19.9 us -> 0.02 us  [on_device(): lax.all_gather(values_local, 'seq', axis=1, tiled=True)]
    all_gather x1, waiting for transfers between devices: 0.02 us -> 19.8 us  [on_device(): lax.all_gather(keys_local, 'seq', axis=1, tiled=True)]
    unnamed x58 -> x54, local copies, waits for them, and re-layouts: 33.7 us -> 32.8 us
  transfers between devices with their start and end apart: 15 -> 17, of which waited for: 12 -> 14; matrix products, arithmetic and copies ran while one was open for 11% -> 10% of each run, Pallas kernels for 0% -> 0%
where the time goes in v1:
time: 1330 us
  waiting for transfers between devices  1050 us (79%)
  matrix products  110 us (8%)
  blocking collectives  64.3 us (5%)
  local copies, waits for them, and re-layouts  42.8 us (3%)
  other arithmetic  42.5 us (3%)
  between operations  15.9 us (1%)
    reduce_scatter x1, waiting for transfers between devices, on_device(): lax.psum_scatter(grad_fc2.astype(jnp.bfloat16), 'fsdp', scatter_dimension...  148 us
    all_gather x1, waiting for transfers between devices, on_device(): lax.all_gather(low_fc1, 'fsdp', axis=0, tiled=True)  147 us
    reduce_scatter x1, waiting for transfers between devices, on_device(): lax.psum_scatter(grad_fc1.astype(jnp.bfloat16), 'fsdp', scatter_dimension...  146 us
    all_gather x1, waiting for transfers between devices, on_device(): lax.all_gather(low_fc2, 'fsdp', axis=0, tiled=True)  141 us
    reduce_scatter x1, waiting for transfers between devices, on_device(): lax.psum_scatter(grad_qkv.astype(jnp.bfloat16), 'fsdp', scatter_dimension...  111 us
    all_gather x1, waiting for transfers between devices, on_device(): lax.all_gather(low_qkv, 'fsdp', axis=0, tiled=True)  90.8 us
    psum x1, waiting for transfers between devices, on_device(): lax.psum(shards[1].astype(jnp.bfloat16), ('rep', 'seq')).astype(jnp.float32)  87.3 us
    reduce_scatter x1, waiting for transfers between devices, on_device(): lax.psum_scatter(grad_out.astype(jnp.bfloat16), 'fsdp', scatter_dimension...  46.8 us
  transfers between devices with their start and end apart: 17, of which 14 were waited for; matrix products, arithmetic and copies ran while one was open for 10% of the time, Pallas kernels for 0%

profile of v1, /device:TPU:0, one launch (start us, length us, event | category | flops | bytes accessed | tf_op | source)
XLA Modules:
  0.0 1325.9 jit_solution(14956507997004816215)
XLA Ops:
  10.7 12.6 all_gather.32
  23.3 14.3 %all_gather.33 = bf16[6,1024]{1,0:T(8,128)(2,1)S(1)} all-gather(bf16[6,256]{1,0:T(8,128)(2,1)S(1)} %convert_element_type.212), channel_id=1, replica_groups=mesh['rep'=4,'fsdp'=4,'seq'=2] {'fsdp'}, dimensions={1}, use_global_device_ids=true | all-gather | bytes 15360 | tf_op jit(solution)/shard_map/all_gather | solution.py:114
  38.1 90.8 %all-gather.9.cloned.1.call-done = bf16[1024,3072]{1,0:T(8,128)(2,1)} async-done(((bf16[256,3072]{1,0:T(8,128)(2,1)}), bf16[1024,3072]{1,0:T(8,128)(2,1)}) %all-gather.9.cloned.1.call-update) | async-done | bytes 6291472 | tf_op jit(solution)/shard_map/all_gather | solution.py:109
  149.0 11.9 all_gather.39
  164.0 19.8 %all-gather.19.cloned.1.call-done = bf16[592,1024]{1,0:T(8,128)(2,1)} async-done(((bf16[296,1024]{1,0:T(8,128)(2,1)}), bf16[592,1024]{1,0:T(8,128)(2,1)}) %all-gather.19.cloned.1.call-update) | async-done | bytes 1212432 | tf_op jit(solution)/shard_map/all_gather | solution.py:144
  197.1 34.1 %all-gather.11.cloned.1.call-done = bf16[1024,1024]{1,0:T(8,128)(2,1)} async-done(((bf16[256,1024]{1,0:T(8,128)(2,1)}), bf16[1024,1024]{1,0:T(8,128)(2,1)}) %all-gather.11.cloned.1.call-update) | async-done | bytes 2097168 | tf_op jit(solution)/shard_map/all_gather | solution.py:110
  234.3 147.1 %all-gather.13.cloned.1.call-done = bf16[1024,4096]{1,0:T(8,128)(2,1)} async-done(((bf16[256,4096]{1,0:T(8,128)(2,1)}), bf16[1024,4096]{1,0:T(8,128)(2,1)}) %all-gather.13.cloned.1.call-update) | async-done | bytes 8388624 | tf_op jit(solution)/shard_map/all_gather | solution.py:111
  381.5 8.6 convolution_add_fusion
  390.1 141.3 %all-gather.15.cloned.1.call-done = bf16[4096,1024]{1,0:T(8,128)(2,1)} async-done(((bf16[1024,1024]{1,0:T(8,128)(2,1)}), bf16[4096,1024]{1,0:T(8,128)(2,1)}) %all-gather.15.cloned.1.call-update) | async-done | bytes 8388624 | tf_op jit(solution)/shard_map/all_gather | solution.py:112
  531.4 9.1 fusion.61
  549.1 8.6 fusion.9
  557.7 6.2 copy.37
  567.2 9.8 multiply_reduce_fusion
  577.0 6.6 multiply_convert_fusion
  586.6 6.2 copy.35
  596.0 5.6 fusion.60
  606.8 9.3 reduce-scatter.25.cloned.1.call-done
  620.1 7.4 convolution_convert_fusion.2
  627.5 110.9 %reduce-scatter.15.cloned.1.call-done = bf16[256,3072]{1,0:T(8,128)(2,1)} async-done(((bf16[1024,3072]{1,0:T(8,128)(2,1)}), bf16[256,3072]{1,0:T(8,128)(2,1)}) %reduce-scatter.15.cloned.1.call-update) | async-done | bytes 1572880 | tf_op jit(solution)/shard_map/reduce_scatter | solution.py:236
  742.3 8.8 convolution_convert_fusion.1
  751.2 10.6 convolution_convert_fusion
  762.0 7.4 fusion.33
  771.3 21.3 %all-reduce.7.cloned.1.call-done = bf16[256,3072]{1,0:T(8,128)(2,1)} async-done(((bf16[256,3072]{1,0:T(8,128)(2,1)}), bf16[256,3072]{1,0:T(8,128)(2,1)}) %all-reduce.7.cloned.1.call-update) | async-done | bytes 1572880 | tf_op jit(solution)/shard_map/psum | solution.py:260
  792.7 46.8 %reduce-scatter.17.cloned.1.call-done = bf16[256,1024]{1,0:T(8,128)(2,1)} async-done(((bf16[1024,1024]{1,0:T(8,128)(2,1)}), bf16[256,1024]{1,0:T(8,128)(2,1)}) %reduce-scatter.17.cloned.1.call-update) | async-done | bytes 524304 | tf_op jit(solution)/shard_map/reduce_scatter | solution.py:239
  839.5 146.0 %reduce-scatter.19.cloned.1.call-done = bf16[256,4096]{1,0:T(8,128)(2,1)} async-done(((bf16[1024,4096]{1,0:T(8,128)(2,1)}), bf16[256,4096]{1,0:T(8,128)(2,1)}) %reduce-scatter.19.cloned.1.call-update) | async-done | bytes 2097168 | tf_op jit(solution)/shard_map/reduce_scatter | solution.py:242
  985.5 147.6 %reduce-scatter.21.cloned.1.call-done = bf16[1024,1024]{1,0:T(8,128)(2,1)} async-done(((bf16[4096,1024]{1,0:T(8,128)(2,1)}), bf16[1024,1024]{1,0:T(8,128)(2,1)}) %reduce-scatter.21.cloned.1.call-update) | async-done | bytes 2097168 | tf_op jit(solution)/shard_map/reduce_scatter | solution.py:245
  1135.0 11.3 all-reduce
  1146.3 8.6 fusion.25
  1157.2 18.9 %reduce-scatter.23.cloned.1.call-done = bf16[6,256]{1,0:T(8,128)(2,1)} async-done(((bf16[6,1024]{1,0:T(8,128)(2,1)}), bf16[6,256]{1,0:T(8,128)(2,1)}) %reduce-scatter.23.cloned.1.call-update) | async-done | bytes 3088 | tf_op jit(solution)/shard_map/reduce_scatter | solution.py:251
  1176.2 14.2 %all-reduce.1 = (bf16[2,256]{1,0:T(2,128)(2,1)S(1)}, bf16[6,256]{1,0:T(8,128)(2,1)S(1)}, bf16[1024]{0:T(1024)(128)(2,1)S(1)}) all-reduce(bf16[2,256]{1,0:T(2,128)(2,1)S(1)} %copy.40, bf16[6,256]{1,0:T(8,128)(2,1)} %reduce-scatter.23.cloned.1.call-done, ...), channel_id=1, replica_groups=mesh['rep'=4,'fsdp'=4,'seq'=2] {'rep','seq'}, use_global_device_ids=true, to_apply=%region_25.26 | all-reduce | flops 3072 | bytes 12288 | tf_op jit(solution)/shard_map/psum | solution.py:268
  1192.2 27.3 %all-reduce.9.cloned.1.call-done = bf16[256,3072]{1,0:T(8,128)(2,1)} async-done(((bf16[256,3072]{1,0:T(8,128)(2,1)}), bf16[256,3072]{1,0:T(8,128)(2,1)}) %all-reduce.9.cloned.1.call-update) | async-done | bytes 1572880 | tf_op jit(solution)/shard_map/psum | solution.py:261
  1223.0 87.3 %all-reduce.11.cloned.1.call-done = (bf16[256,1024]{1,0:T(8,128)(2,1)}, bf16[256,4096]{1,0:T(8,128)(2,1)}, bf16[1024,1024]{1,0:T(8,128)(2,1)}) async-done(((bf16[256,1024]{1,0:T(8,128)(2,1)}, bf16[256,4096]{1,0:T(8,128)(2,1)}, bf16[1024,1024]{1,0:T(8,128)(2,1)}), (bf16[256,1024]{1,0:T(8,128)(2,1)}, bf16[256,4096]{1,0:T(8,128)(2,1)}, bf16[1024,1024]{1,0:T(8,128)(2,1)})) %all-reduce.11.cloned.1.call-update) | async-done | bytes 4718608 | tf_op jit(solution)/shard_map/psum | solution.py:265
  (147 shorter events, 93.4 us)
Async XLA Ops:
  7.2 3.5 copy-start.15
  7.2 3.5 copy-start.17
  7.2 30.4 %copy-start.2 = (bf16[1,296,1024]{2,1,0:T(8,128)(2,1)S(1)}, bf16[1,296,1024]{2,1,0:T(8,128)(2,1)}, u32[]{:S(2)}) copy-start(bf16[1,296,1024]{2,1,0:T(8,128)(2,1)} %param.10) | copy-start | bytes 1818628
  7.2 121.7 %all-gather.9.cloned.1.call-start = ((), (), s32[]{:S(2)}) async-start(), calls=%async_computation.8 | async-start | bytes 7864320 | tf_op jit(solution)/shard_map/all_gather | solution.py:109
  10.6 150.8 %all-gather.17.cloned.1.call-start = ((), (), s32[]{:S(2)}) async-start(), calls=%async_computation.19 | async-start | bytes 1818624 | tf_op jit(solution)/shard_map/all_gather | solution.py:145
  137.0 46.9 %all-gather.19.cloned.1.call-start = ((), (), s32[]{:S(2)}) async-start(), calls=%async_computation.20 | async-start | bytes 1818624 | tf_op jit(solution)/shard_map/all_gather | solution.py:144
  139.3 91.9 %all-gather.11.cloned.1.call-start = ((), (), s32[]{:S(2)}) async-start(), calls=%async_computation.9 | async-start | bytes 2621440 | tf_op jit(solution)/shard_map/all_gather | solution.py:110
  140.2 241.2 %all-gather.13.cloned.1.call-start = ((), (), s32[]{:S(2)}) async-start(), calls=%async_computation.10 | async-start | bytes 10485760 | tf_op jit(solution)/shard_map/all_gather | solution.py:111
  144.4 387.0 %all-gather.15.cloned.1.call-start = ((), (), s32[]{:S(2)}) async-start(), calls=%async_computation.11 | async-start | bytes 10485760 | tf_op jit(solution)/shard_map/all_gather | solution.py:112
  148.3 453.3 %reduce-scatter.27.cloned.1.call-start = ((), (), s32[]{:S(2)}) async-start(), calls=%async_computation.22 | async-start | bytes 1818624
  161.3 24.2 %copy-start.5 = (bf16[296,1024]{0,1:T(8,128)(2,1)}, bf16[296,1024]{0,1:T(8,128)(2,1)S(1)}, u32[]{:S(2)}) copy-start(bf16[296,1024]{0,1:T(8,128)(2,1)S(1)} %copy.32) | copy-start | bytes 1818628
  187.8 4.8 copy-start
  187.8 4.8 copy-start.7
  531.4 9.1 copy-start.18
  540.4 3.1 copy-start.20
  540.5 3.1 copy-start.13
  567.1 49.1 %reduce-scatter.25.cloned.1.call-start = ((), (), s32[]{:S(2)}) async-start(), calls=%async_computation.21 | async-start | bytes 1818624
  577.0 6.6 copy-start.6
  596.0 142.5 %reduce-scatter.15.cloned.1.call-start = ((), (), s32[]{:S(2)}) async-start(), calls=%async_computation.12 | async-start | bytes 7864320 | tf_op jit(solution)/shard_map/reduce_scatter | solution.py:236
  627.5 111.1 %copy-start.4 = (f32[296,1024]{1,0:T(8,128)S(1)}, f32[296,1024]{1,0:T(8,128)}, u32[]{:S(2)}) copy-start(f32[296,1024]{1,0:T(8,128)} %copy-done.3) | copy-start | bytes 3637252
  627.5 165.1 %all-reduce.7.cloned.1.call-start = ((), (), s32[]{:S(2)}) async-start(), calls=%async_computation.13 | async-start | bytes 3145728 | tf_op jit(solution)/shard_map/psum | solution.py:260
  738.5 101.0 %reduce-scatter.17.cloned.1.call-start = ((), (), s32[]{:S(2)}) async-start(), calls=%async_computation.15 | async-start | bytes 2621440 | tf_op jit(solution)/shard_map/reduce_scatter | solution.py:239
  742.2 243.3 %reduce-scatter.19.cloned.1.call-start = ((), (), s32[]{:S(2)}) async-start(), calls=%async_computation.16 | async-start | bytes 10485760 | tf_op jit(solution)/shard_map/reduce_scatter | solution.py:242
  751.1 382.0 %reduce-scatter.21.cloned.1.call-start = ((), (), s32[]{:S(2)}) async-start(), calls=%async_computation.17 | async-start | bytes 10485760 | tf_op jit(solution)/shard_map/reduce_scatter | solution.py:245
  761.8 394.6 %reduce-scatter.29.cloned.1.call-start = ((), (), s32[]{:S(2)}) async-start(), calls=%async_computation.23 | async-start | bytes 327680
  770.4 405.8 %reduce-scatter.23.cloned.1.call-start = ((), (), s32[]{:S(2)}) async-start(), calls=%async_computation.18 | async-start | bytes 20480 | tf_op jit(solution)/shard_map/reduce_scatter | solution.py:251
  771.2 448.3 %all-reduce.9.cloned.1.call-start = ((), (), s32[]{:S(2)}) async-start(), calls=%async_computation.14 | async-start | bytes 3145728 | tf_op jit(solution)/shard_map/psum | solution.py:261
  792.6 517.7 %all-reduce.11.cloned.1.call-start = ((), (), s32[]{:S(2)}) async-start(), calls=%async_computation.24 | async-start | bytes 9437184 | tf_op jit(solution)/shard_map/psum | solution.py:265
  1146.3 8.7 copy-start.14
  1146.3 8.7 copy-start.11
  1155.0 21.2 %dynamic-slice-start = ((bf16[4096]{0:T(1024)(128)(2,1)}, u32[]{:T(128)}), bf16[1024]{0:T(1024)(128)(2,1)S(1)}, s32[]{:S(2)}) async-start(bf16[4096]{0:T(1024)(128)(2,1)} %copy-done.14, u32[]{:T(128)} %multiply.49), calls=%async_computation.25 | async-start | bytes 4608
  1312.4 4.3 copy-start.9
  (7 other events, 11.3 us)
Sparse Core Ops, SparseCore 0:
  10.7 118.1 all-gather.8
  137.1 21.4 all-gather.16
  160.7 23.1 all-gather.18
  185.3 45.9 all-gather.10
  233.2 148.2 all-gather.12
  383.5 147.8 all-gather.14
  567.2 20.3 reduce-scatter.26
  596.1 20.0 reduce-scatter.24
  627.6 110.7 reduce-scatter.14
  740.6 51.9 all-reduce.6
  795.6 43.8 reduce-scatter.16
  841.7 143.7 reduce-scatter.18
  987.9 145.1 reduce-scatter.20
  1135.8 20.3 reduce-scatter.28
  1158.9 17.1 reduce-scatter.22
  1178.4 41.0 all-reduce.8
  1223.0 87.2 all-reduce.10
